TPU v7x, 512 devices: a whole 4x8x8 slice. The times are simulated.
512 devices in a mesh: ctx: 64 (over y, z_hi, core), fsdp: 8 (over z_lo, x).
Axes of the slice: x: 4, y: 8, z: 8 (z_hi: 4, z_lo: 2; z = z_hi * 2 + z_lo), core: 2. Of those that a mesh axis runs over, the one named last changes fastest.
Arguments:
- query_act: bfloat16 [16384, 3072], P('ctx', 'fsdp'), may hold values from -10 to 10
- key_act: bfloat16 [16384, 3072], P('ctx', 'fsdp'), may hold values from -4 to 4
- value_act: bfloat16 [16384, 3072], P('ctx', 'fsdp'), may hold values from -6 to 6
- resid_in: bfloat16 [16384, 3072], P('ctx', 'fsdp'), may hold values from -60 to 60
- gate_vec: float32 [3072], P('fsdp'), may hold values from 0.5 to 2.5
- mod_scale: float32 [3072], P('fsdp'), may hold values from -2.5 to 2.5
- mod_shift: float32 [3072], P('fsdp'), may hold values from -3 to 3
- w_up: bfloat16 [3072, 6912], P(('ctx', 'fsdp')), may hold values from -0.109375 to 0.109375
- bias_up: float32 [6912], P('fsdp'), may hold values from -3 to 3
Outputs:
- residual: bfloat16 [16384, 3072], P('ctx', 'fsdp')
- hidden: bfloat16 [16384, 6912], P('ctx', 'fsdp')
All inputs are finite; a program needn't handle non-finite values.
Results may differ from a plain program's by a relative error of at most 0.0059.
Values may be sent and summed in bfloat16 or wider, within the bound.
A program may use at most 64 MiB of HBM per device.

v0:
```python
import math
import jax
import jax.numpy as jnp
from jax import lax
from jax.sharding import PartitionSpec as P

HEAD = 128
D = 3072


def padded_2(cells, sides, width):
    for axis, dim in sides:
        count = lax.axis_size(axis)
        ends = count - 1
        head = lax.slice_in_dim(cells, 0, width, axis=dim)
        tail = lax.slice_in_dim(cells, cells.shape[dim] - width, cells.shape[dim], axis=dim)
        cells = jnp.concatenate(
            [
                lax.ppermute(tail, axis, [(i, (i + 1) % count) for i in range(ends)]),
                cells,
                lax.ppermute(head, axis, [((i + 1) % count, i) for i in range(ends)]),
            ],
            axis=dim,
        )
    return cells


def shards(query_act, key_act, value_act, resid_in, gate_vec, mod_scale, mod_shift, w_up, bias_up):
    tok_rows = query_act.shape[0]
    feat_width = query_act.shape[1]
    reach_rows = tok_rows // 2
    ctx_count = lax.axis_size("ctx")
    seq_total = tok_rows * ctx_count
    stacked = jnp.stack([key_act, value_act])
    padded = padded_2(stacked, (("ctx", 1),), reach_rows)
    first_pos = lax.axis_index("ctx") * tok_rows
    query_pos = first_pos + jnp.arange(tok_rows, dtype=jnp.int32)
    key_pos = first_pos - reach_rows + jnp.arange(tok_rows + 2 * reach_rows, dtype=jnp.int32)
    allowed = (
        (jnp.abs(query_pos[:, None] - key_pos[None, :]) <= reach_rows)
        & (key_pos[None, :] >= 0)
        & (key_pos[None, :] < seq_total)
    )
    scale_qk = 1.0 / math.sqrt(HEAD)
    head_outputs = []
    for head_idx in range(feat_width // HEAD):
        head_cols = slice(head_idx * HEAD, (head_idx + 1) * HEAD)
        scores = (
            jnp.einsum(
                "qd,kd->qk",
                query_act[:, head_cols],
                padded[0, :, head_cols],
                preferred_element_type=jnp.float32,
            )
            * scale_qk
        )
        masked = jnp.where(allowed, scores, -jnp.inf)
        row_max = jnp.max(masked, axis=1, keepdims=True)
        exp_terms = jnp.exp(masked - row_max)
        attn_probs = (exp_terms / jnp.sum(exp_terms, axis=1, keepdims=True)).astype(jnp.bfloat16)
        head_outputs.append(
            jnp.dot(attn_probs, padded[1, :, head_cols], preferred_element_type=jnp.float32)
        )
    attended = jnp.concatenate(head_outputs, axis=1).astype(jnp.bfloat16)
    residual_out = (resid_in.astype(jnp.float32) + gate_vec * attended.astype(jnp.float32)).astype(
        jnp.bfloat16
    )
    rows_float = residual_out.astype(jnp.float32)
    row_sum = lax.psum(jnp.sum(rows_float, axis=1), "fsdp")
    mean_val = row_sum / D
    centered = rows_float - mean_val[:, None]
    var_val = lax.psum(jnp.sum(centered * centered, axis=1), "fsdp") / D
    normed = (
        centered * lax.rsqrt(var_val + 1e-06)[:, None] * (1.0 + mod_scale) + mod_shift
    ).astype(jnp.bfloat16)
    full_feat = lax.all_gather(normed, "fsdp", axis=1, tiled=True)
    strided = lax.all_gather(w_up, "ctx", axis=0, tiled=True)
    regrouped = lax.all_to_all(strided, "fsdp", split_axis=1, concat_axis=0, tiled=True)
    fsdp_count = lax.axis_size("fsdp")
    row_width = w_up.shape[0]
    permuted = (
        full_feat.reshape(tok_rows, ctx_count, fsdp_count, row_width)
        .transpose(0, 2, 1, 3)
        .reshape(tok_rows, -1)
    )
    pre_act = jnp.dot(permuted, regrouped, preferred_element_type=jnp.float32)
    hidden = jax.nn.gelu(pre_act + bias_up, approximate=True).astype(jnp.bfloat16)
    return (residual_out, hidden)


def solution(mesh):
    placed = (
        P("ctx", "fsdp"),
        P("ctx", "fsdp"),
        P("ctx", "fsdp"),
        P("ctx", "fsdp"),
        P("fsdp"),
        P("fsdp"),
        P("fsdp"),
        P(("ctx", "fsdp"), None),
        P("fsdp"),
    )
    return jax.shard_map(
        shards,
        mesh=mesh,
        in_specs=placed,
        out_specs=(P("ctx", "fsdp"), P("ctx", "fsdp")),
        check_vma=False,
    )
```

profile of v0, /device:TPU:8, one launch (start us, length us, event | category | flops | bytes accessed | tf_op | source)
XLA Modules:
  0.0 307.6 jit_solution(431408384966726718)
XLA Ops:
  8.0 0.7 all-gather.6.cloned.1.call-update
  8.7 106.1 %all-gather.6.cloned.1.call-done = bf16[64,6,6912]{2,1,0:T(8,128)(2,1)} async-done(((bf16[1,6,6912]{2,1,0:T(8,128)(2,1)}), bf16[64,6,6912]{2,1,0:T(8,128)(2,1)}) %all-gather.6.cloned.1.call-update) | async-done | bytes 5308432 | tf_op jit(solution)/shard_map/all_gather | solution.py:77
  114.8 13.9 %all_to_all.14 = bf16[384,8,864]{2,1,0:T(8,128)(2,1)} reshape(bf16[64,6,6912]{2,1,0:T(8,128)(2,1)} %all-gather.6.cloned.1.call-done) | data formatting | bytes 10616832 | tf_op jit(solution)/shard_map/all_to_all | solution.py:78
  128.7 8.4 %copy.19 = bf16[384,8,864]{0,2,1:T(8,128)(2,1)} copy(bf16[384,8,864]{2,1,0:T(8,128)(2,1)} %all_to_all.14) | data formatting | bytes 10616832 | tf_op jit(solution)/shard_map/all_to_all | solution.py:78
  137.2 4.8 %all-to-all-start = ((bf16[384,8,864]{0,2,1:T(8,128)(2,1)}), bf16[384,8,864]{0,2,1:T(8,128)(2,1)}, u32[]{:S(2)}, u32[]{:S(2)}) async-start(bf16[384,8,864]{0,2,1:T(8,128)(2,1)} %copy.19), calls=%async_computation | async-start | bytes 10616832 | tf_op jit(solution)/shard_map/all_to_all | solution.py:78
  142.1 2.2 collective-permute-start
  144.3 6.4 %collective-permute-start.1 = (bf16[2,128,384]{2,1,0:T(8,128)(2,1)S(1)}, bf16[2,128,384]{2,1,0:T(8,128)(2,1)S(1)}, u32[]{:S(2)}, u32[]{:S(2)}) collective-permute-start(bf16[2,128,384]{2,1,0:T(8,128)(2,1)S(1)} %get-tuple-element.11), channel_id=1, source_target_pairs={{8,0},{16,8},{24,16},{32,24},{40,32},{48,40},{56,48},{64,56},{72,6... | collective-permute-start | bytes 589832 | tf_op jit(solution)/shard_map/ppermute | solution.py:21
  150.8 0.1 copy.17
  151.0 3.2 %collective-permute-done = bf16[2,128,384]{2,1,0:T(8,128)(2,1)S(1)} collective-permute-done((bf16[2,128,384]{2,1,0:T(8,128)(2,1)S(1)}, bf16[2,128,384]{2,1,0:T(8,128)(2,1)S(1)}, u32[]{:S(2)}, u32[]{:S(2)}) %collective-permute-start) | collective-permute-done | bytes 196640 | tf_op jit(solution)/shard_map/ppermute | solution.py:19
  154.2 0.1 pad_maximum_fusion
  154.3 0.3 fusion.31
  154.6 0.1 fusion.20
  154.7 0.3 fusion.32
  155.1 0.1 fusion.19
  155.2 0.3 fusion.33
  155.5 0.1 fusion.18
  155.7 0.3 convolution_convert_fusion
  155.9 0.3 convolution_convert_fusion.1
  156.2 0.3 convolution_convert_fusion.2
  156.5 0.4 copy-done.3
  156.9 0.2 convert_reduce_fusion
  157.0 60.3 %psum.14 = f32[256]{0:T(256)S(1)} all-reduce(f32[256]{0:T(256)S(1)} %get-tuple-element.8), channel_id=1, replica_groups=mesh['ctx'=64,'fsdp'=8] {'fsdp'}, use_global_device_ids=true, to_apply=%region_7.8 | all-reduce | flops 256 | bytes 2048 | tf_op jit(solution)/shard_map/psum | solution.py:69
  217.4 0.1 fusion.21
  217.5 18.2 %psum.15 = f32[256]{0:T(256)S(1)} all-reduce(f32[256]{0:T(256)S(1)} %fusion.21), channel_id=1, replica_groups=mesh['ctx'=64,'fsdp'=8] {'fsdp'}, use_global_device_ids=true, to_apply=%region_9.10 | all-reduce | flops 256 | bytes 2048 | tf_op jit(solution)/shard_map/psum | solution.py:72
  235.7 0.9 fusion.24
  236.6 0.8 copy.21
  237.4 50.2 %all-gather.4.cloned.1.call-done = bf16[256,3072]{0,1:T(8,128)(2,1)} async-done(((bf16[256,384]{0,1:T(8,128)(2,1)}), bf16[256,3072]{0,1:T(8,128)(2,1)}) %all-gather.4.cloned.1.call-update) | async-done | bytes 1572880 | tf_op jit(solution)/shard_map/all_gather | solution.py:76
  287.6 2.5 reshape.41
  290.1 1.5 copy.18
  291.6 2.6 reshape.42
  294.2 3.5 %copy.22 = bf16[8,108,8,384]{3,2,0,1:T(8,128)(2,1)S(1)} copy(bf16[8,108,8,384]{3,2,1,0:T(8,128)(2,1)} %bitcast.14) | data formatting | bytes 10616832 | tf_op jit(solution)/shard_map/all_to_all | solution.py:78
  297.7 2.5 fusion.13
  (27 shorter events, 0.2 us)
Async XLA Ops:
  8.0 106.8 %all-gather.6.cloned.1.call-start = ((), (), s32[]{:S(2)}) async-start(), calls=%async_computation.2 | async-start | bytes 7188480 | tf_op jit(solution)/shard_map/all_gather | solution.py:77
  137.2 4.9 %copy-start = (bf16[256,384]{1,0:T(8,128)(2,1)S(1)}, bf16[256,384]{1,0:T(8,128)(2,1)}, u32[]{:S(2)}) copy-start(bf16[256,384]{1,0:T(8,128)(2,1)} %param.10) | copy-start | bytes 589828
  137.2 4.9 %copy-start.1 = (bf16[256,384]{1,0:T(8,128)(2,1)S(1)}, bf16[256,384]{1,0:T(8,128)(2,1)}, u32[]{:S(2)}) copy-start(bf16[256,384]{1,0:T(8,128)(2,1)} %param.11) | copy-start | bytes 589828
  137.2 13.6 %copy-start.2 = (bf16[256,384]{1,0:T(8,128)(2,1)S(1)}, bf16[256,384]{1,0:T(8,128)(2,1)}, u32[]{:S(2)}) copy-start(bf16[256,384]{1,0:T(8,128)(2,1)} %param.12) | copy-start | bytes 589828
  137.2 13.8 %copy-start.5 = (f32[384]{0:T(512)S(1)}, f32[384]{0:T(512)}, u32[]{:S(2)}) copy-start(f32[384]{0:T(512)} %param.14) | copy-start | bytes 4612
  137.2 157.0 %all-to-all-start = ((bf16[384,8,864]{0,2,1:T(8,128)(2,1)}), bf16[384,8,864]{0,2,1:T(8,128)(2,1)}, u32[]{:S(2)}, u32[]{:S(2)}) async-start(bf16[384,8,864]{0,2,1:T(8,128)(2,1)} %copy.19), calls=%async_computation | async-start | bytes 10616832 | tf_op jit(solution)/shard_map/all_to_all | solution.py:78
  142.0 12.2 %copy-start.6 = (bf16[256,384]{1,0:T(8,128)(2,1)S(1)}, bf16[256,384]{1,0:T(8,128)(2,1)}, u32[]{:S(2)}) copy-start(bf16[256,384]{1,0:T(8,128)(2,1)} %param.9) | copy-start | bytes 589828
  142.0 145.6 %all-gather.4.cloned.1.call-start = ((), (), s32[]{:S(2)}) async-start(), calls=%async_computation.1 | async-start | bytes 1769472 | tf_op jit(solution)/shard_map/all_gather | solution.py:76
  142.1 12.0 %collective-permute-start = (bf16[2,128,384]{2,1,0:T(8,128)(2,1)S(1)}, bf16[2,128,384]{2,1,0:T(8,128)(2,1)S(1)}, u32[]{:S(2)}, u32[]{:S(2)}) collective-permute-start(bf16[2,128,384]{2,1,0:T(8,128)(2,1)S(1)} %get-tuple-element.10), channel_id=1, source_target_pairs={{0,8},{8,16},{16,24},{24,32},{32,40},{40,48},{48,56},{56,64},{64,7... | collective-permute-start | bytes 589832 | tf_op jit(solution)/shard_map/ppermute | solution.py:19
  144.3 9.9 %collective-permute-start.1 = (bf16[2,128,384]{2,1,0:T(8,128)(2,1)S(1)}, bf16[2,128,384]{2,1,0:T(8,128)(2,1)S(1)}, u32[]{:S(2)}, u32[]{:S(2)}) collective-permute-start(bf16[2,128,384]{2,1,0:T(8,128)(2,1)S(1)} %get-tuple-element.11), channel_id=1, source_target_pairs={{8,0},{16,8},{24,16},{32,24},{40,32},{48,40},{56,48},{64,56},{72,6... | collective-permute-start | bytes 589832 | tf_op jit(solution)/shard_map/ppermute | solution.py:21
  156.2 0.7 copy-start.3
  156.2 79.5 %copy-start.4 = (f32[384]{0:T(512)S(1)}, f32[384]{0:T(512)}, u32[]{:S(2)}) copy-start(f32[384]{0:T(512)} %param.15) | copy-start | bytes 4612
  294.2 3.5 %copy-start.7 = (f32[864]{0:T(1024)S(1)}, f32[864]{0:T(1024)}, u32[]{:S(2)}) copy-start(f32[864]{0:T(1024)} %param.17) | copy-start | bytes 10372
Sparse Core Ops, SparseCore 0:
  12.1 102.6 all-gather.5
Sparse Core Ops, SparseCore 1:
  236.7 50.9 all-gather.3
where the time goes:
time: 308 us
  waiting for transfers between devices  160 us (52%)
  blocking collectives  78.5 us (25%)
  local copies, waits for them, and re-layouts  33.8 us (11%)
  between operations  15.7 us (5%)
  starting transfers between devices  13.5 us (4%)
  matrix products  4.25 us (1%)
    all_gather x1, waiting for transfers between devices, shards(): strided = lax.all_gather(w_up, 'ctx', axis=0, tiled=True)  106 us
    psum x1, blocking collectives, shards(): row_sum = lax.psum(jnp.sum(rows_float, axis=1), 'fsdp')  60.3 us
    all_gather x1, waiting for transfers between devices, shards(): full_feat = lax.all_gather(normed, 'fsdp', axis=1, tiled=True)  50.2 us
    all_to_all x3, local copies, waits for them, and re-layouts, shards(): lax.all_to_all(strided, 'fsdp', split_axis=1, concat_axis=0, tiled=True)  25.9 us
    psum x1, blocking collectives, shards(): var_val = lax.psum(jnp.sum(centered * centered, axis=1), 'fsdp') / D  18.2 us
    ppermute x1, starting transfers between devices, padded_2(): lax.ppermute(head, axis, [((i + 1) % count, i) for i in range(ends)])  6.43 us
  transfers between devices with their start and end apart: 5, of which 3 were waited for; matrix products, arithmetic and copies ran while one was open for 4% of the time, Pallas kernels for 0%

commit v1 on v0

--- a/solution.py
+++ b/solution.py
@@ -74,7 +74,9 @@
         centered * lax.rsqrt(var_val + 1e-06)[:, None] * (1.0 + mod_scale) + mod_shift
     ).astype(jnp.bfloat16)
     full_feat = lax.all_gather(normed, "fsdp", axis=1, tiled=True)
-    strided = lax.all_gather(w_up, "ctx", axis=0, tiled=True)
+    strided = jnp.concatenate(
+        lax.all_to_all(jnp.stack([w_up] * lax.axis_size("ctx")), "ctx", 0, 0), axis=0
+    )
     regrouped = lax.all_to_all(strided, "fsdp", split_axis=1, concat_axis=0, tiled=True)
     fsdp_count = lax.axis_size("fsdp")
     row_width = w_up.shape[0]

time: 308 us -> 393 us (1.28)
  blocking collectives: 78.5 us -> 259 us
  waiting for transfers between devices: 160 us -> 68.8 us
  starting transfers between devices: 13.5 us -> 9.21 us
    all_to_all x0 -> x1, blocking collectives: none -> 182 us  [shards(): lax.all_to_all(jnp.stack([w_up] * lax.axis_size('ctx')), 'ctx', 0, 0)]
    all_gather x1 -> x0, waiting for transfers between devices: 106 us -> none  [shards(): strided = lax.all_gather(w_up, 'ctx', axis=0, tiled=True)]
    all_gather x1, waiting for transfers between devices: 50.2 us -> 59.9 us  [shards(): full_feat = lax.all_gather(normed, 'fsdp', axis=1, tiled=True)]
    ppermute x1, waiting for transfers between devices: 3.18 us -> 8.41 us  [padded_2(): lax.ppermute(tail, axis, [(i, (i + 1) % count) for i in range(ends)])]
    ppermute x1, starting transfers between devices: 6.43 us -> 1.92 us  [padded_2(): lax.ppermute(head, axis, [((i + 1) % count, i) for i in range(ends)])]
  transfers between devices with their start and end apart: 5 -> 4, of which waited for: 3 -> 3; matrix products, arithmetic and copies ran while one was open for 4% -> 3% of each run, Pallas kernels for 0% -> 0%
where the time goes in v1:
time: 393 us; the launch traced here: 392 us
  blocking collectives  259 us (66%)
  waiting for transfers between devices  68.8 us (18%)
  local copies, waits for them, and re-layouts  35.2 us (9%)
  between operations  14.3 us (4%)
  starting transfers between devices  9.21 us (2%)
  matrix products  4.25 us (1%)
    all_to_all x1, blocking collectives, shards(): lax.all_to_all(jnp.stack([w_up] * lax.axis_size('ctx')), 'ctx', 0, 0)  182 us
    all_gather x1, waiting for transfers between devices, shards(): full_feat = lax.all_gather(normed, 'fsdp', axis=1, tiled=True)  59.9 us
    psum x1, blocking collectives, shards(): row_sum = lax.psum(jnp.sum(rows_float, axis=1), 'fsdp')  58.7 us
    all_to_all x3, local copies, waits for them, and re-layouts, shards(): lax.all_to_all(strided, 'fsdp', split_axis=1, concat_axis=0, tiled=True)  25.9 us
    psum x1, blocking collectives, shards(): var_val = lax.psum(jnp.sum(centered * centered, axis=1), 'fsdp') / D  18.2 us
    ppermute x1, waiting for transfers between devices, padded_2(): lax.ppermute(tail, axis, [(i, (i + 1) % count) for i in range(ends)])  8.41 us
  transfers between devices with their start and end apart: 4, of which 3 were waited for; matrix products, arithmetic and copies ran while one was open for 3% of the time, Pallas kernels for 0%

profile of v1, /device:TPU:8, one launch (start us, length us, event | category | flops | bytes accessed | tf_op | source)
XLA Modules:
  0.0 392.0 jit_solution(4904293495325251307)
XLA Ops:
  7.2 1.4 stack.11
  8.5 181.8 %all_to_all.24 = bf16[64,6,6912]{2,1,0:T(8,128)(2,1)} all-to-all(bf16[64,6,6912]{2,1,0:T(8,128)(2,1)S(1)} %stack.11), channel_id=1, replica_groups=mesh['ctx'=64,'fsdp'=8] {'ctx'}, dimensions={0} | all-to-all | bytes 10616832 | tf_op jit(solution)/shard_map/all_to_all | solution.py:78
  190.3 13.9 %all_to_all.18 = bf16[384,8,864]{2,1,0:T(8,128)(2,1)} reshape(bf16[64,6,6912]{2,1,0:T(8,128)(2,1)} %all_to_all.24) | data formatting | bytes 10616832 | tf_op jit(solution)/shard_map/all_to_all | solution.py:80
  204.2 8.4 %copy.19 = bf16[384,8,864]{0,2,1:T(8,128)(2,1)} copy(bf16[384,8,864]{2,1,0:T(8,128)(2,1)} %all_to_all.18) | data formatting | bytes 10616832 | tf_op jit(solution)/shard_map/all_to_all | solution.py:80
  212.7 4.8 %all-to-all-start.1 = ((bf16[384,8,864]{0,2,1:T(8,128)(2,1)}), bf16[384,8,864]{0,2,1:T(8,128)(2,1)}, u32[]{:S(2)}, u32[]{:S(2)}) async-start(bf16[384,8,864]{0,2,1:T(8,128)(2,1)} %copy.19), calls=%async_computation.1 | async-start | bytes 10616832 | tf_op jit(solution)/shard_map/all_to_all | solution.py:80
  217.7 1.9 collective-permute-start.1
  219.6 2.4 collective-permute-start
  222.0 0.1 copy.17
  222.3 0.5 collective-permute-done.1
  222.8 8.4 %collective-permute-done = bf16[2,128,384]{2,1,0:T(8,128)(2,1)S(1)} collective-permute-done((bf16[2,128,384]{2,1,0:T(8,128)(2,1)S(1)}, bf16[2,128,384]{2,1,0:T(8,128)(2,1)S(1)}, u32[]{:S(2)}, u32[]{:S(2)}) %collective-permute-start) | collective-permute-done | bytes 196640 | tf_op jit(solution)/shard_map/ppermute | solution.py:19
  231.3 0.3 fusion.31
  231.6 0.1 fusion.20
  231.7 0.3 fusion.32
  232.1 0.1 fusion.19
  232.2 0.3 fusion.33
  232.6 0.1 fusion.18
  232.7 0.3 convolution_convert_fusion
  232.9 0.3 convolution_convert_fusion.1
  233.2 0.3 convolution_convert_fusion.2
  233.5 0.4 copy-done.3
  233.9 0.2 convert_reduce_fusion
  234.0 58.7 %psum.14 = f32[256]{0:T(256)S(1)} all-reduce(f32[256]{0:T(256)S(1)} %get-tuple-element.8), channel_id=1, replica_groups=mesh['ctx'=64,'fsdp'=8] {'fsdp'}, use_global_device_ids=true, to_apply=%region_7.8 | all-reduce | flops 256 | bytes 2048 | tf_op jit(solution)/shard_map/psum | solution.py:69
  292.7 0.1 fusion.21
  292.8 18.2 %psum.15 = f32[256]{0:T(256)S(1)} all-reduce(f32[256]{0:T(256)S(1)} %fusion.21), channel_id=1, replica_groups=mesh['ctx'=64,'fsdp'=8] {'fsdp'}, use_global_device_ids=true, to_apply=%region_9.10 | all-reduce | flops 256 | bytes 2048 | tf_op jit(solution)/shard_map/psum | solution.py:72
  311.0 0.9 fusion.24
  311.9 0.8 copy.21
  312.7 59.9 %all-gather.2.cloned.1.call-done = bf16[256,3072]{0,1:T(8,128)(2,1)} async-done(((bf16[256,384]{0,1:T(8,128)(2,1)}), bf16[256,3072]{0,1:T(8,128)(2,1)}) %all-gather.2.cloned.1.call-update) | async-done | bytes 1572880 | tf_op jit(solution)/shard_map/all_gather | solution.py:76
  372.6 2.5 reshape.45
  375.1 1.5 copy.18
  376.6 2.6 reshape.46
  379.2 3.5 copy.22
  382.7 2.5 fusion.13
  (26 shorter events, 0.3 us)
Async XLA Ops:
  212.7 4.9 %copy-start = (bf16[256,384]{1,0:T(8,128)(2,1)S(1)}, bf16[256,384]{1,0:T(8,128)(2,1)}, u32[]{:S(2)}) copy-start(bf16[256,384]{1,0:T(8,128)(2,1)} %param.10) | copy-start | bytes 589828
  212.7 4.9 %copy-start.1 = (bf16[256,384]{1,0:T(8,128)(2,1)S(1)}, bf16[256,384]{1,0:T(8,128)(2,1)}, u32[]{:S(2)}) copy-start(bf16[256,384]{1,0:T(8,128)(2,1)} %param.11) | copy-start | bytes 589828
  212.7 9.3 %copy-start.2 = (bf16[256,384]{1,0:T(8,128)(2,1)S(1)}, bf16[256,384]{1,0:T(8,128)(2,1)}, u32[]{:S(2)}) copy-start(bf16[256,384]{1,0:T(8,128)(2,1)} %param.12) | copy-start | bytes 589828
  212.7 9.5 %copy-start.5 = (f32[384]{0:T(512)S(1)}, f32[384]{0:T(512)}, u32[]{:S(2)}) copy-start(f32[384]{0:T(512)} %param.14) | copy-start | bytes 4612
  212.7 166.4 %all-to-all-start.1 = ((bf16[384,8,864]{0,2,1:T(8,128)(2,1)}), bf16[384,8,864]{0,2,1:T(8,128)(2,1)}, u32[]{:S(2)}, u32[]{:S(2)}) async-start(bf16[384,8,864]{0,2,1:T(8,128)(2,1)} %copy.19), calls=%async_computation.1 | async-start | bytes 10616832 | tf_op jit(solution)/shard_map/all_to_all | solution.py:80
  217.5 13.7 %copy-start.6 = (bf16[256,384]{1,0:T(8,128)(2,1)S(1)}, bf16[256,384]{1,0:T(8,128)(2,1)}, u32[]{:S(2)}) copy-start(bf16[256,384]{1,0:T(8,128)(2,1)} %param.9) | copy-start | bytes 589828
  217.6 155.1 %all-gather.2.cloned.1.call-start = ((), (), s32[]{:S(2)}) async-start(), calls=%async_computation.2 | async-start | bytes 1769472 | tf_op jit(solution)/shard_map/all_gather | solution.py:76
  217.7 5.1 %collective-permute-start.1 = (bf16[2,128,384]{2,1,0:T(8,128)(2,1)S(1)}, bf16[2,128,384]{2,1,0:T(8,128)(2,1)S(1)}, u32[]{:S(2)}, u32[]{:S(2)}) collective-permute-start(bf16[2,128,384]{2,1,0:T(8,128)(2,1)S(1)} %get-tuple-element.11), channel_id=1, source_target_pairs={{8,0},{16,8},{24,16},{32,24},{40,32},{48,40},{56,48},{64,56},{72,6... | collective-permute-start | bytes 589832 | tf_op jit(solution)/shard_map/ppermute | solution.py:21
  219.6 11.6 %collective-permute-start = (bf16[2,128,384]{2,1,0:T(8,128)(2,1)S(1)}, bf16[2,128,384]{2,1,0:T(8,128)(2,1)S(1)}, u32[]{:S(2)}, u32[]{:S(2)}) collective-permute-start(bf16[2,128,384]{2,1,0:T(8,128)(2,1)S(1)} %get-tuple-element.10), channel_id=1, source_target_pairs={{0,8},{8,16},{16,24},{24,32},{32,40},{40,48},{48,56},{56,64},{64,7... | collective-permute-start | bytes 589832 | tf_op jit(solution)/shard_map/ppermute | solution.py:19
  233.2 0.7 copy-start.3
  233.2 77.8 %copy-start.4 = (f32[384]{0:T(512)S(1)}, f32[384]{0:T(512)}, u32[]{:S(2)}) copy-start(f32[384]{0:T(512)} %param.15) | copy-start | bytes 4612
  379.2 3.5 copy-start.7
Sparse Core Ops, SparseCore 0:
  312.0 60.5 all-gather.1
